TPU v7x, 32 devices: a whole 2x2x4 slice. The times are simulated.
32 devices in a mesh: tok: 4 (over z), hid: 8 (over y, x, core).
Axes of the slice: x: 2, y: 2, z: 4, core: 2. Of those that a mesh axis runs over, the one named last changes fastest.
Arguments:
- tokens: bfloat16 [4096, 8192], P('tok', 'hid'), may hold values from -6 to 6
- qkv_weight: bfloat16 [8192, 10240], P('tok', 'hid'), may hold values from -0.09375 to 0.09375
- qkv_cotangent: bfloat16 [4096, 10240], P('tok', 'hid'), may hold values from -6 to 6
Outputs:
- projected: bfloat16 [4096, 10240], P('tok', 'hid')
- input_grad: bfloat16 [4096, 8192], P('tok', 'hid')
- weight_grad: bfloat16 [8192, 10240], P('tok', 'hid')
All inputs are finite; a program needn't handle non-finite values.
Results may differ from a plain program's by a relative error of at most 0.012.
Values may be sent and summed in bfloat16 or wider, within the bound.
A program may use at most 192 MiB of HBM per device.

v0:
```python
import jax
import jax.numpy as jnp
from jax import lax
from jax.sharding import PartitionSpec as P


def local(tokens, qkv_weight, qkv_cotangent):
    local_rows = tokens.shape[0]
    full_rows = lax.all_gather(tokens, "hid", axis=1, tiled=True)
    segment = lax.all_gather(qkv_weight, "tok", axis=0, tiled=True)
    features = full_rows
    summed = jnp.dot(features, segment, preferred_element_type=jnp.float32)
    backward = lax.dot_general(
        qkv_cotangent, segment, (((1,), (1,)), ((), ())), preferred_element_type=jnp.float32
    )
    partial_grad = backward.astype(jnp.bfloat16)
    summed, partial_grad = (summed, partial_grad)
    projected = summed.astype(jnp.bfloat16)
    input_grad = (
        lax.psum_scatter(partial_grad, "hid", scatter_dimension=1, tiled=True)
        .astype(jnp.float32)
        .astype(jnp.bfloat16)
    )
    factor = float(local_rows * lax.axis_size("tok")) ** (-0.5)
    features = full_rows
    grad_block = lax.psum_scatter(
        lax.dot_general(
            features, qkv_cotangent, (((0,), (0,)), ((), ())), preferred_element_type=jnp.float32
        ).astype(jnp.bfloat16),
        "tok",
        scatter_dimension=0,
        tiled=True,
    ).astype(jnp.float32)
    weight_grad = (grad_block * factor).astype(jnp.bfloat16)
    return (projected, input_grad, weight_grad)


def solution(mesh):
    in_specs = (P("tok", "hid"), P("tok", "hid"), P("tok", "hid"))
    out_specs = (P("tok", "hid"), P("tok", "hid"), P("tok", "hid"))
    return jax.shard_map(local, mesh=mesh, in_specs=in_specs, out_specs=out_specs, check_vma=False)
```

profile of v0, /device:TPU:0, one launch (start us, length us, event | category | flops | bytes accessed | tf_op | source)
XLA Modules:
  0.0 937.1 jit_solution(6630098638862187927)
XLA Ops:
  7.2 0.0 copy-start
  7.2 0.0 all-gather.3.cloned.1.call-start
  7.2 0.7 all-gather.3.cloned.1.call-update
  7.9 0.0 all-gather.5.cloned.1.call-start
  8.0 0.7 all-gather.5.cloned.1.call-update
  8.7 0.0 reduce-scatter.5.cloned.1.call-start
  8.7 93.7 %all-gather.3.cloned.1.call-done = bf16[1024,8192]{1,0:T(8,128)(2,1)} async-done(((bf16[1024,1024]{1,0:T(8,128)(2,1)}), bf16[1024,8192]{1,0:T(8,128)(2,1)}) %all-gather.3.cloned.1.call-update) | async-done | bytes 16777232 | tf_op jit(solution)/shard_map/all_gather | solution.py:9
  102.4 0.0 copy-done
  102.4 31.9 %convolution_convert_fusion = bf16[8192,1280]{1,0:T(8,128)(2,1)} fusion(bf16[1024,8192]{1,0:T(8,128)(2,1)} %all-gather.3.cloned.1.call-done, bf16[1024,1280]{1,0:T(8,128)(2,1)S(1)} %copy-done), kind=kOutput, calls=%fused_computation | convolution fusion | flops 21485322240 | bytes 40370176 | tf_op jit(solution)/shard_map/dot_general | solution.py:27
  134.2 0.0 reduce-scatter.5.cloned.1.call-update
  134.3 0.2 reduce-scatter.3.cloned.1.call-start
  134.5 326.3 %all-gather.5.cloned.1.call-done = bf16[8192,1280]{1,0:T(8,128)(2,1)} async-done(((bf16[2048,1280]{1,0:T(8,128)(2,1)}), bf16[8192,1280]{1,0:T(8,128)(2,1)}) %all-gather.5.cloned.1.call-update) | async-done | bytes 20971536 | tf_op jit(solution)/shard_map/all_gather | solution.py:10
  460.8 27.2 %convolution_convert_fusion.1 = bf16[1024,8192]{1,0:T(8,128)(2,1)} fusion(bf16[1024,1280]{1,0:T(8,128)(2,1)S(1)} %copy-done, bf16[8192,1280]{1,0:T(8,128)(2,1)} %all-gather.5.cloned.1.call-done), kind=kOutput, calls=%fused_computation.1 | convolution fusion | flops 21483225088 | bytes 40370176 | tf_op jit(solution)/shard_map/dot_general | solution.py:13
  488.0 0.0 reduce-scatter.3.cloned.1.call-update
  488.0 0.0 copy-start.1
  488.0 28.1 %convolution_convert_fusion.2 = bf16[1024,1280]{1,0:T(8,128)(2,1)} fusion(bf16[1024,8192]{1,0:T(8,128)(2,1)} %all-gather.3.cloned.1.call-done, bf16[8192,1280]{1,0:T(8,128)(2,1)} %all-gather.5.cloned.1.call-done), kind=kOutput, calls=%fused_computation.3 | convolution fusion | flops 21476147200 | bytes 40370176 | tf_op jit(solution)/shard_map/dot_general | solution.py:12
  516.1 293.1 %reduce-scatter.5.cloned.1.call-done = bf16[2048,1280]{1,0:T(8,128)(2,1)} async-done(((bf16[8192,1280]{1,0:T(8,128)(2,1)}), bf16[2048,1280]{1,0:T(8,128)(2,1)}) %reduce-scatter.5.cloned.1.call-update) | async-done | bytes 5242896 | tf_op jit(solution)/shard_map/reduce_scatter | solution.py:26
  809.2 5.8 multiply_convert_fusion
  815.0 115.5 %reduce-scatter.3.cloned.1.call-done = bf16[1024,1024]{1,0:T(8,128)(2,1)} async-done(((bf16[1024,8192]{1,0:T(8,128)(2,1)}), bf16[1024,1024]{1,0:T(8,128)(2,1)}) %reduce-scatter.3.cloned.1.call-update) | async-done | bytes 2097168 | tf_op jit(solution)/shard_map/reduce_scatter | solution.py:20
  930.5 0.0 copy-done.1
Async XLA Ops:
  7.2 95.2 %copy-start = (bf16[1024,1280]{1,0:T(8,128)(2,1)S(1)}, bf16[1024,1280]{1,0:T(8,128)(2,1)}, u32[]{:S(2)}) copy-start(bf16[1024,1280]{1,0:T(8,128)(2,1)} %param.5) | copy-start | bytes 7864324
  7.2 95.2 %all-gather.3.cloned.1.call-start = ((), (), s32[]{:S(2)}) async-start(), calls=%async_computation.2 | async-start | bytes 18874368 | tf_op jit(solution)/shard_map/all_gather | solution.py:9
  7.9 452.9 %all-gather.5.cloned.1.call-start = ((), (), s32[]{:S(2)}) async-start(), calls=%async_computation.3 | async-start | bytes 26214400 | tf_op jit(solution)/shard_map/all_gather | solution.py:10
  8.7 800.5 %reduce-scatter.5.cloned.1.call-start = ((), (), s32[]{:S(2)}) async-start(), calls=%async_computation.5 | async-start | bytes 26214400 | tf_op jit(solution)/shard_map/reduce_scatter | solution.py:26
  134.3 796.2 %reduce-scatter.3.cloned.1.call-start = ((), (), s32[]{:S(2)}) async-start(), calls=%async_computation.4 | async-start | bytes 18874368 | tf_op jit(solution)/shard_map/reduce_scatter | solution.py:20
  488.0 442.5 %copy-start.1 = (bf16[1024,1280]{1,0:T(8,128)(2,1)S(1)}, bf16[1024,1280]{1,0:T(8,128)(2,1)}, u32[]{:S(2)}) copy-start(bf16[1024,1280]{1,0:T(8,128)(2,1)} %param.5) | copy-start | bytes 7864324
Sparse Core Ops, SparseCore 0:
  9.9 92.4 all-gather.2
  104.0 356.8 all-gather.4
  463.2 345.9 reduce-scatter.4
  813.1 117.3 reduce-scatter.2
where the time goes:
time: 937 us
  waiting for transfers between devices  830 us (89%)
  matrix products  87.1 us (9%)
  between operations  13.8 us (1%)
    all_gather x1, waiting for transfers between devices, local(): segment = lax.all_gather(qkv_weight, 'tok', axis=0, tiled=True)  326 us
    reduce_scatter x1, waiting for transfers between devices, local(): lax.psum_scatter(lax.dot_general(features, qkv_cotangent, (((0,), (0,)),...  293 us
    reduce_scatter x1, waiting for transfers between devices, local(): lax.psum_scatter(partial_grad, 'hid', scatter_dimension=1, tiled=True)  116 us
    all_gather x1, waiting for transfers between devices, local(): full_rows = lax.all_gather(tokens, 'hid', axis=1, tiled=True)  93.7 us
    dot_general x1, matrix products, local(): lax.dot_general(features, qkv_cotangent, (((0,), (0,)), ((), ())), prefer...  31.9 us
    dot_general x1, matrix products, local(): summed = jnp.dot(features, segment, preferred_element_type=jnp.float32)  28.1 us
    dot_general x1, matrix products, local(): lax.dot_general(qkv_cotangent, segment, (((1,), (1,)), ((), ())), preferr...  27.2 us
  transfers between devices with their start and end apart: 4, of which 4 were waited for; matrix products, arithmetic and copies ran while one was open for 10% of the time, Pallas kernels for 0%

commit v1 on v0

--- a/solution.py
+++ b/solution.py
@@ -7,7 +7,9 @@
 def local(tokens, qkv_weight, qkv_cotangent):
     local_rows = tokens.shape[0]
     full_rows = lax.all_gather(tokens, "hid", axis=1, tiled=True)
-    segment = lax.all_gather(qkv_weight, "tok", axis=0, tiled=True)
+    segment = jnp.concatenate(
+        lax.all_to_all(jnp.stack([qkv_weight] * lax.axis_size("tok")), "tok", 0, 0), axis=0
+    )
     features = full_rows
     summed = jnp.dot(features, segment, preferred_element_type=jnp.float32)
     backward = lax.dot_general(

time: 937 us -> 1080 us (1.15)
  blocking collectives: 0 us -> 791 us
  waiting for transfers between devices: 830 us -> 176 us
    all_to_all x0 -> x1, blocking collectives: none -> 791 us  [local(): lax.all_to_all(jnp.stack([qkv_weight] * lax.axis_size('tok')), 'tok', 0, 0)]
    all_gather x1 -> x0, waiting for transfers between devices: 326 us -> none  [local(): segment = lax.all_gather(qkv_weight, 'tok', axis=0, tiled=True)]
    reduce_scatter x1, waiting for transfers between devices: 293 us -> 0.01 us  [local(): lax.psum_scatter(lax.dot_general(features, qkv_cotangent, (((0,), (0,)),...]
    reduce_scatter x1, waiting for transfers between devices: 116 us -> 81.3 us  [local(): lax.psum_scatter(partial_grad, 'hid', scatter_dimension=1, tiled=True)]
  transfers between devices with their start and end apart: 4 -> 3, of which waited for: 4 -> 2; matrix products, arithmetic and copies ran while one was open for 10% -> 6% of each run, Pallas kernels for 0% -> 0%
where the time goes in v1:
time: 1080 us
  blocking collectives  791 us (73%)
  waiting for transfers between devices  176 us (16%)
  matrix products  87 us (8%)
  between operations  13.8 us (1%)
    all_to_all x1, blocking collectives, local(): lax.all_to_all(jnp.stack([qkv_weight] * lax.axis_size('tok')), 'tok', 0, 0)  791 us
    all_gather x1, waiting for transfers between devices, local(): full_rows = lax.all_gather(tokens, 'hid', axis=1, tiled=True)  94.4 us
    reduce_scatter x1, waiting for transfers between devices, local(): lax.psum_scatter(partial_grad, 'hid', scatter_dimension=1, tiled=True)  81.3 us
    dot_general x1, matrix products, local(): lax.dot_general(features, qkv_cotangent, (((0,), (0,)), ((), ())), prefer...  32 us
    dot_general x1, matrix products, local(): summed = jnp.dot(features, segment, preferred_element_type=jnp.float32)  28.1 us
    dot_general x1, matrix products, local(): lax.dot_general(qkv_cotangent, segment, (((1,), (1,)), ((), ())), preferr...  26.9 us
  transfers between devices with their start and end apart: 3, of which 2 were waited for; matrix products, arithmetic and copies ran while one was open for 6% of the time, Pallas kernels for 0%

profile of v1, /device:TPU:0, one launch (start us, length us, event | category | flops | bytes accessed | tf_op | source)
XLA Modules:
  0.0 1078.7 jit_solution(16915964440779842357)
XLA Ops:
  7.2 0.0 copy-start
  7.2 0.0 all-gather.2.cloned.1.call-start
  7.2 0.7 all-gather.2.cloned.1.call-update
  7.9 0.0 reduce-scatter.5.cloned.1.call-start
  8.0 94.4 %all-gather.2.cloned.1.call-done = bf16[1024,8192]{1,0:T(8,128)(2,1)} async-done(((bf16[1024,1024]{1,0:T(8,128)(2,1)}), bf16[1024,8192]{1,0:T(8,128)(2,1)}) %all-gather.2.cloned.1.call-update) | async-done | bytes 16777232 | tf_op jit(solution)/shard_map/all_gather | solution.py:9
  102.4 0.0 copy-done
  102.4 32.0 %convolution_convert_fusion = bf16[8192,1280]{1,0:T(8,128)(2,1)} fusion(bf16[1024,8192]{1,0:T(8,128)(2,1)} %all-gather.2.cloned.1.call-done, bf16[1024,1280]{1,0:T(8,128)(2,1)S(1)} %copy-done), kind=kOutput, calls=%fused_computation | convolution fusion | flops 21485322240 | bytes 40370176 | tf_op jit(solution)/shard_map/dot_general | solution.py:29
  134.4 0.0 reduce-scatter.5.cloned.1.call-update
  134.4 0.0 reduce-scatter.3.cloned.1.call-start
  134.5 5.0 stack.2
  139.4 790.6 %all_to_all.5 = bf16[4,2048,1280]{2,1,0:T(8,128)(2,1)} all-to-all(bf16[4,2048,1280]{2,1,0:T(8,128)(2,1)S(1)} %stack.2), channel_id=1, replica_groups=mesh['tok'=4,'hid'=8] {'tok'}, dimensions={0} | all-to-all | bytes 41943040 | tf_op jit(solution)/shard_map/all_to_all | solution.py:11
  930.0 26.9 %convolution_convert_fusion.1 = bf16[1024,8192]{1,0:T(8,128)(2,1)} fusion(bf16[1024,1280]{1,0:T(8,128)(2,1)S(1)} %copy-done, bf16[8192,1280]{1,0:T(8,128)(2,1)} %bitcast.7), kind=kOutput, calls=%fused_computation.1 | convolution fusion | flops 21483225088 | bytes 40370176 | tf_op jit(solution)/shard_map/dot_general | solution.py:15
  956.9 0.0 reduce-scatter.3.cloned.1.call-update
  957.0 0.0 copy-start.1
  957.0 28.1 %convolution_convert_fusion.2 = bf16[1024,1280]{1,0:T(8,128)(2,1)} fusion(bf16[1024,8192]{1,0:T(8,128)(2,1)} %all-gather.2.cloned.1.call-done, bf16[8192,1280]{1,0:T(8,128)(2,1)} %bitcast.8), kind=kOutput, calls=%fused_computation.3 | convolution fusion | flops 21476147200 | bytes 40370176 | tf_op jit(solution)/shard_map/dot_general | solution.py:14
  985.0 0.0 reduce-scatter.5.cloned.1.call-done
  985.0 5.8 multiply_convert_fusion
  990.9 81.3 %reduce-scatter.3.cloned.1.call-done = bf16[1024,1024]{1,0:T(8,128)(2,1)} async-done(((bf16[1024,8192]{1,0:T(8,128)(2,1)}), bf16[1024,1024]{1,0:T(8,128)(2,1)}) %reduce-scatter.3.cloned.1.call-update) | async-done | bytes 2097168 | tf_op jit(solution)/shard_map/reduce_scatter | solution.py:22
  1072.1 0.0 copy-done.1
Async XLA Ops:
  7.2 95.2 %copy-start = (bf16[1024,1280]{1,0:T(8,128)(2,1)S(1)}, bf16[1024,1280]{1,0:T(8,128)(2,1)}, u32[]{:S(2)}) copy-start(bf16[1024,1280]{1,0:T(8,128)(2,1)} %param.5) | copy-start | bytes 7864324
  7.2 95.2 %all-gather.2.cloned.1.call-start = ((), (), s32[]{:S(2)}) async-start(), calls=%async_computation.3 | async-start | bytes 18874368 | tf_op jit(solution)/shard_map/all_gather | solution.py:9
  7.9 977.1 %reduce-scatter.5.cloned.1.call-start = ((), (), s32[]{:S(2)}) async-start(), calls=%async_computation.5 | async-start | bytes 26214400 | tf_op jit(solution)/shard_map/reduce_scatter | solution.py:28
  134.4 937.7 %reduce-scatter.3.cloned.1.call-start = ((), (), s32[]{:S(2)}) async-start(), calls=%async_computation.4 | async-start | bytes 18874368 | tf_op jit(solution)/shard_map/reduce_scatter | solution.py:22
  957.0 115.2 %copy-start.1 = (bf16[1024,1280]{1,0:T(8,128)(2,1)S(1)}, bf16[1024,1280]{1,0:T(8,128)(2,1)}, u32[]{:S(2)}) copy-start(bf16[1024,1280]{1,0:T(8,128)(2,1)} %param.5) | copy-start | bytes 7864324
Sparse Core Ops, SparseCore 0:
  9.9 92.4 all-gather.1
  134.5 717.3 reduce-scatter.4
  957.1 115.0 reduce-scatter.2
